TPU v7x, 32 devices: a whole 2x2x4 slice. The times are simulated.
32 devices in a mesh: pair: 8 (over y, x, core), idx: 4 (over z).
Axes of the slice: x: 2, y: 2, z: 4, core: 2. Of those that a mesh axis runs over, the one named last changes fastest.
Arguments:
- g2: bfloat16 [512, 512, 2, 1, 512], P('pair', None, None, None, 'idx'), may hold values from -6 to 6
- core_ham: float32 [512, 512], replicated, may hold values from -0.25 to 0.25
- dipole: float32 [512, 512], replicated, may hold values from -0.125 to 0.125
- field: float32 [1], replicated, may hold values from 0.5 to 1.5
- rho: bfloat16 [2, 512, 512], replicated, may hold values from -6 to 6
- factors: bfloat16 [2048, 512, 512], P(None, 'pair', 'idx'), may hold values from -0.046875 to 0.046875
- damping: float32 [512], replicated, may hold values from 0.02 to 0.2
Outputs:
- g2_next: bfloat16 [512, 512, 2, 1, 512], P('pair', None, None, None, 'idx')
All inputs are finite; a program needn't handle non-finite values.
Results may differ from a plain program's by a relative error of at most 0.0056.
Values may be sent and summed in bfloat16 or wider, within the bound.
A program may use at most 384 MiB of HBM per device.

v0:
```python
import jax
import jax.numpy as jnp
from jax import lax
from jax.sharding import PartitionSpec as P


def combine(total_x, total_z, rho_part):
    real = (
        total_z[:, 0, None, None] * rho_part[0][None]
        - total_z[:, 1, None, None] * rho_part[1][None]
    )
    imag = (
        total_z[:, 0, None, None] * rho_part[1][None]
        + total_z[:, 1, None, None] * rho_part[0][None]
    )
    return total_x + jnp.stack([real, imag], axis=1)


def per_device(g2, core_ham, dipole, field, rho, factors, damping):
    step_size = 1.0
    rows_loc, width, _, slab, cols_loc = g2.shape
    rank = factors.shape[0]
    kcols = factors.shape[2]
    pair_pos = lax.axis_index("pair")
    idx_pos = lax.axis_index("idx")
    hamil = 0.5 * (core_ham + core_ham.T) + field[0] * (0.5 * (dipole + dipole.T))
    ham_b = hamil.astype(jnp.bfloat16)
    part = lax.all_to_all(g2, "pair", split_axis=1, concat_axis=0, tiled=True)
    shape = part.shape
    mixed = jnp.dot(ham_b, part.reshape(shape[0], -1), preferred_element_type=jnp.float32)
    mixed = mixed.astype(jnp.bfloat16).reshape(shape)
    term_i = lax.all_to_all(mixed, "pair", split_axis=0, concat_axis=1, tiled=True)
    wide = lax.all_to_all(g2, "idx", split_axis=1, concat_axis=4, tiled=True)
    lmat = factors.reshape(rank, -1)
    rho_rows = lax.dynamic_slice_in_dim(rho, pair_pos * rows_loc, rows_loc, 1)
    slab_rho = rho[:, :slab, :].astype(jnp.float32)
    rho_local = lax.dynamic_slice_in_dim(rho_rows, idx_pos * kcols, kcols, 2).reshape(2, -1)
    part_x = jnp.dot(lmat, wide.reshape(rows_loc * kcols, -1), preferred_element_type=jnp.float32)
    part_z = lax.dot_general(
        lmat, rho_local, (((1,), (1,)), ((), ())), preferred_element_type=jnp.float32
    )
    total_x, total_z = lax.psum((part_x, part_z), ("pair", "idx"))
    aux = combine(total_x.reshape(rank, 2, slab, width), total_z, slab_rho).astype(jnp.bfloat16)
    ham_cols = jnp.dot(wide.reshape(-1, width), ham_b, preferred_element_type=jnp.float32).reshape(
        wide.shape
    )
    factor_term = lax.dot_general(
        lmat, aux.reshape(rank, -1), (((0,), (0,)), ((), ())), preferred_element_type=jnp.float32
    )
    part_two = (factor_term.reshape(wide.shape) - ham_cols).astype(jnp.bfloat16)
    term_two = lax.all_to_all(part_two, "idx", split_axis=4, concat_axis=1, tiled=True)
    term_k = jnp.einsum(
        "km,imr->ikr", ham_b, g2.reshape(rows_loc, width, -1), preferred_element_type=jnp.float32
    ).reshape(g2.shape)
    values = g2.astype(jnp.float32)
    slab_ham = ham_b[:slab, :slab].astype(jnp.float32)
    term_j = slab_ham[:, 0][None, None, None, :, None] * values
    rate = term_i.astype(jnp.float32) + term_two.astype(jnp.float32) + term_j - term_k
    gam_rows = lax.dynamic_slice_in_dim(damping, pair_pos * rows_loc, rows_loc, 0)
    gam_cols = lax.dynamic_slice_in_dim(damping, idx_pos * cols_loc, cols_loc, 0)
    decay = (
        gam_rows[:, None, None, None]
        + damping[None, :, None, None]
        + damping[:slab][None, None, :, None]
        + gam_cols[None, None, None, :]
    )
    real_next = values[:, :, 0] + step_size * rate[:, :, 1] - step_size * decay * values[:, :, 0]
    imag_next = values[:, :, 1] - step_size * rate[:, :, 0] - step_size * decay * values[:, :, 1]
    return jnp.stack([real_next, imag_next], axis=2).astype(jnp.bfloat16)


def solution(mesh):
    placed = (P("pair", None, None, None, "idx"), P(), P(), P(), P(), P(None, "pair", "idx"), P())
    return jax.shard_map(
        per_device,
        mesh=mesh,
        in_specs=placed,
        out_specs=P("pair", None, None, None, "idx"),
        check_vma=False,
    )
```

profile of v0, /device:TPU:0, one launch (start us, length us, event | category | flops | bytes accessed | tf_op | source)
XLA Modules:
  0.0 1787.3 jit_solution(3607498592157163440)
XLA Ops:
  6.5 17.1 copy.83
  29.4 188.9 %all_to_all.48 = bf16[64,512,2,1,128]{4,2,3,0,1:T(2,128)(2,1)} all-to-all(bf16[64,512,2,1,128]{4,2,3,0,1:T(2,128)(2,1)S(1)} %copy.83), channel_id=1, replica_groups=mesh['pair'=8,'idx'=4] {'pair'}, dimensions={1} | all-to-all | bytes 33554432 | tf_op jit(solution)/shard_map/all_to_all | solution.py:28
  229.9 17.2 fusion.18
  247.1 360.5 %psum.15 = f32[2048,2]{0,1:T(2,128)S(1)} all-reduce(f32[2048,2]{0,1:T(2,128)S(1)} %fusion.18), channel_id=1, replica_groups=mesh['pair'=8,'idx'=4] {'pair','idx'}, use_global_device_ids=true, to_apply=%region_1.0 | all-reduce | flops 4096 | bytes 32768 | tf_op jit(solution)/shard_map/psum | solution.py:42
  614.2 18.2 %copy.134 = bf16[64,8,64,2,1,128]{5,3,2,0,1,4:T(2,128)(2,1)} copy(bf16[64,8,64,2,1,128]{5,3,0,2,1,4:T(2,128)(2,1)} %bitcast.93) | data formatting | bytes 33554432 | tf_op jit(solution)/shard_map/all_to_all | solution.py:28
  632.4 27.8 %reshape.414 = bf16[512,16384]{1,0:T(8,128)(2,1)} reshape(bf16[8,64,64,2,1,128]{5,3,2,1,0,4:T(2,128)(2,1)} %bitcast.95) | data formatting | bytes 33554432 | tf_op jit(solution)/shard_map/reshape | solution.py:30
  660.2 18.2 %convolution_convert_fusion = bf16[512,16384]{1,0:T(8,128)(2,1)} fusion(bf16[512,512]{1,0:T(8,128)(2,1)S(1)} %fusion.23, bf16[512,16384]{1,0:T(8,128)(2,1)} %reshape.414), kind=kOutput, calls=%fused_computation.14 | convolution fusion | flops 8598323200 | bytes 34078720 | tf_op jit(solution)/shard_map/dot_general | solution.py:30
  678.4 27.4 %reshape.415 = bf16[512,64,2,1,128]{4,2,1,0,3:T(2,128)(2,1)} reshape(bf16[512,16384]{1,0:T(8,128)(2,1)} %convolution_convert_fusion) | data formatting | bytes 33554432 | tf_op jit(solution)/shard_map/reshape | solution.py:31
  711.8 42.7 %copy.135 = bf16[64,4,128,2,1,128]{5,1,3,2,0,4:T(4,128)(2,1)} copy(bf16[64,4,128,2,1,128]{5,3,0,2,1,4:T(2,128)(2,1)} %bitcast.9) | data formatting | bytes 33554432 | tf_op jit(solution)/shard_map/all_to_all | solution.py:33
  754.5 27.4 %reshape.430 = bf16[8192,1024]{1,0:T(8,128)(2,1)} reshape(bf16[64,128,2,1,4,128]{5,4,2,1,0,3:T(4,128)(2,1)} %bitcast.85) | data formatting | bytes 33554432 | tf_op jit(solution)/shard_map/reshape | solution.py:38
  781.9 45.0 %fusion.2 = f32[2048,1024]{1,0:T(8,128)} fusion(bf16[8192,1024]{1,0:T(8,128)(2,1)} %reshape.430, bf16[256,8,64,128]{3,2,1,0:T(8,128)(2,1)} %bitcast.87), kind=kOutput, calls=%fused_computation.2 | convolution fusion | flops 34359738368 | bytes 58720256 | tf_op jit(solution)/shard_map/dot_general | solution.py:38
  853.5 23.5 %convolution_bitcast_fusion = f32[16384,512]{0,1:T(8,128)} fusion(bf16[512,512]{1,0:T(8,128)(2,1)S(1)} %fusion.23, bf16[2048,8,4,128]{3,2,1,0:T(4,128)(2,1)} %bitcast.86), kind=kOutput, calls=%fused_computation.13 | convolution fusion | flops 8589934592 | bytes 50855936 | tf_op jit(solution)/shard_map/dot_general | solution.py:44
  877.0 33.7 %copy.94 = f32[16384,512]{1,0:T(8,128)} copy(f32[16384,512]{0,1:T(8,128)} %convolution_bitcast_fusion) | data formatting | bytes 67108864 | tf_op jit(solution)/shard_map/dot_general | solution.py:44
  910.6 38.7 %reshape.420 = f32[64,128,2,1,512]{4,2,1,0,3:T(2,128)} reshape(f32[16384,512]{1,0:T(8,128)} %copy.94) | data formatting | bytes 67108864 | tf_op jit(solution)/shard_map/reshape | solution.py:44
  949.3 80.5 %all-reduce.2.cloned.1.call-done = f32[2048,1024]{1,0:T(8,128)} async-done(((f32[2048,1024]{1,0:T(8,128)}), f32[2048,1024]{1,0:T(8,128)}) %all-reduce.2.cloned.1.call-update) | async-done | bytes 8388624 | tf_op jit(solution)/shard_map/psum | solution.py:42
  1029.8 50.2 %fusion.15 = f32[128,8,64,128]{3,1,2,0:T(8,128)} fusion(bf16[256,8,64,128]{3,2,1,0:T(8,128)(2,1)} %bitcast.88, f32[2048,1024]{1,0:T(8,128)} %all-reduce.2.cloned.1.call-done, f32[2048,1024]{1,0:T(8,128)} %copy.93), kind=kOutput, calls=%fused_computation.27 | convolution fusion | flops 34363932672 | bytes 83886080 | tf_op jit(solution)/shard_map/dot_general | solution.py:47
  1080.0 27.8 %copy.106 = f32[128,8,64,128]{3,2,1,0:T(8,128)} copy(f32[128,8,64,128]{3,1,2,0:T(8,128)} %fusion.15) | data formatting | bytes 67108864
  1107.8 34.1 %copy.95 = f32[64,128,2,1,512]{4,1,3,2,0:T(8,128)} copy(f32[64,128,2,1,512]{1,0,4,2,3:T(8,128)} %bitcast.89) | data formatting | bytes 67108864 | tf_op jit(solution)/shard_map/reshape | solution.py:50
  1141.9 28.6 %fusion.4 = bf16[64,128,2,1,512]{4,1,3,2,0:T(8,128)(2,1)} fusion(f32[64,128,2,1,512]{4,1,3,2,0:T(8,128)} %copy.95, f32[64,128,2,1,512]{4,2,1,0,3:T(2,128)} %reshape.420), kind=kLoop, calls=%fused_computation.7 | loop fusion | flops 16777216 | bytes 83886080 | tf_op jit(solution)/shard_map/convert_element_type | solution.py:50
  1170.6 23.2 %copy.97 = bf16[64,128,2,1,512]{1,0,3,2,4:T(8,128)(2,1)} copy(bf16[64,128,2,1,512]{4,1,3,2,0:T(8,128)(2,1)} %fusion.4) | data formatting | bytes 33554432 | tf_op jit(solution)/shard_map/convert_element_type | solution.py:50
  1200.8 40.8 %copy.103 = bf16[64,512,2,1,128]{1,4,2,0,3:T(8,128)(2,1)} copy(bf16[64,512,2,1,128]{4,2,3,1,0:T(2,128)(2,1)} %param.7) | data formatting | bytes 33554432 | tf_op jit(solution)/shard_map/reshape | solution.py:53
  1243.5 17.5 convert_element_type.79
  1260.9 21.4 %fusion.25 = f32[512,64,256]{0,2,1:T(8,128)} fusion(bf16[64,512,256]{1,2,0:T(8,128)(2,1)} %bitcast.92, bf16[512,512]{1,0:T(8,128)(2,1)S(1)} %copy-done.2), kind=kOutput, calls=%fused_computation.39 | convolution fusion | flops 8589934592 | bytes 50855936 | tf_op jit(solution)/shard_map/km,imr->ikr/dot_general | solution.py:52
  1282.3 48.5 %copy.100 = f32[64,512,2,1,128]{4,2,3,1,0:T(2,128)} copy(f32[64,512,2,1,128]{1,4,2,0,3:T(8,128)} %bitcast.84) | data formatting | bytes 67108864 | tf_op jit(solution)/shard_map/reshape | solution.py:54
  1332.2 17.6 convert_bitcast_fusion.1
  1349.8 23.0 %copy.86 = f32[64,8,64,2,1,128]{5,3,2,1,0,4:T(2,128)} copy(f32[64,8,64,2,1,128]{5,3,2,0,1,4:T(2,128)} %convert_bitcast_fusion.1) | data formatting | bytes 67108864 | tf_op jit(solution)/shard_map/convert_element_type | solution.py:58
  1372.8 190.9 %all-to-all-done.3 = bf16[64,128,2,1,512]{1,0,3,2,4:T(8,128)(2,1)} async-done(((bf16[64,128,2,1,512]{1,0,3,2,4:T(8,128)(2,1)}), bf16[64,128,2,1,512]{1,0,3,2,4:T(8,128)(2,1)}, u32[]{:S(2)}, u32[]{:S(2)}) %all-to-all-start.3) | async-done | bytes 16777248 | tf_op jit(solution)/shard_map/all_to_all | solution.py:51
  1563.7 18.7 %convert_bitcast_fusion = f32[64,4,128,2,1,128]{2,0,3,5,1,4:T(8,128)} fusion(bf16[64,128,2,1,4,128]{1,0,2,5,4,3:T(8,128)(2,1)} %bitcast.31), kind=kLoop, calls=%fused_computation.4 | loop fusion | flops 8388608 | bytes 50331648 | tf_op jit(solution)/shard_map/convert_element_type | solution.py:58
  1582.3 38.4 %copy.98 = f32[64,4,128,2,1,128]{5,3,2,1,0,4:T(2,128)} copy(f32[64,4,128,2,1,128]{2,0,3,5,1,4:T(8,128)} %convert_bitcast_fusion) | data formatting | bytes 67108864 | tf_op jit(solution)/shard_map/convert_element_type | solution.py:58
  1620.7 47.8 %add_subtract_fusion = f32[64,512,2,1,128]{4,2,3,1,0:T(2,128)} fusion(f32[64,512,2,1,128]{4,2,3,1,0:T(2,128)} %copy.100, f32[64,512,2,1,128]{4,2,3,1,0:T(2,128)} %bitcast.90, f32[64,512,2,1,128]{4,2,3,1,0:T(2,128)} %bitcast.91, f32[]{:T(128)S(6)} %convert.17, bf16[64,512,2,1,128]{4,2,3,1,0:T(2,128)(2,1)} %param.7), kind=kLoop, calls=%fused_computation.10 | loop fusion | flops 41943040 | bytes 150994944 | tf_op jit(solution)/shard_map/sub | solution.py:58
  1668.5 70.8 %fusion.14 = (bf16[64,512,1,1,128]{4,2,3,1,0:T(2,128)(2,1)S(1)}, bf16[64,512,1,1,128]{4,2,3,1,0:T(2,128)(2,1)}) fusion(f32[64,512,2,1,128]{4,2,3,1,0:T(2,128)} %add_subtract_fusion, f32[64,512,2,1,128]{4,2,3,1,0:T(2,128)} %convert_element_type.79, f32[128]{0:T(128)S(1)} %copy-done.6, f32[64,512]{1,0:T(8,128)S(1)} %add_add_fusion), kind=kLoop, calls=%fused_computation.26 | loop fusion | flops 37748736 | bytes 84017664 | tf_op jit(solution)/shard_map/convert.7
  1739.3 40.7 %pad_maximum_fusion = bf16[64,512,2,1,128]{4,2,3,1,0:T(2,128)(2,1)} fusion(bf16[64,512,1,1,128]{4,2,3,1,0:T(2,128)(2,1)} %get-tuple-element.6, bf16[64,512,1,1,128]{4,2,3,1,0:T(2,128)(2,1)S(1)} %get-tuple-element.5), kind=kLoop, calls=%fused_computation.23 | loop fusion | flops 33554432 | bytes 33554432 | tf_op jit(solution)/shard_map/stack | solution.py:69
  (37 shorter events, 65.3 us)
Async XLA Ops:
  23.7 5.7 copy-start
  218.4 7.2 copy-start.4
  218.4 8.6 copy-start.3
  218.4 487.5 %all-to-all-start.2 = ((bf16[64,512,2,1,128]{4,2,3,0,1:T(2,128)(2,1)}), bf16[64,512,2,1,128]{4,2,3,0,1:T(2,128)(2,1)}, u32[]{:S(2)}, u32[]{:S(2)}) async-start(bf16[64,512,2,1,128]{4,2,3,0,1:T(2,128)(2,1)} %copy-done), calls=%async_computation.2 | async-start | bytes 33554432 | tf_op jit(solution)/shard_map/all_to_all | solution.py:33
  610.4 243.1 %copy-start.1 = (bf16[512,512]{1,0:T(8,128)(2,1)}, bf16[512,512]{1,0:T(8,128)(2,1)S(1)}, u32[]{:S(2)}) copy-start(bf16[512,512]{1,0:T(8,128)(2,1)S(1)} %fusion.23) | copy-start | bytes 1572868
  705.8 487.9 %all-to-all-start.1 = ((bf16[512,64,2,1,128]{4,2,1,3,0:T(2,128)(2,1)}), bf16[512,64,2,1,128]{4,2,1,3,0:T(2,128)(2,1)}, u32[]{:S(2)}, u32[]{:S(2)}) async-start(bf16[512,64,2,1,128]{4,2,1,3,0:T(2,128)(2,1)} %bitcast.94), calls=%async_computation.1 | async-start | bytes 33554432 | tf_op jit(solution)/shard_map/all_to_all | solution.py:32
  711.6 318.2 %all-reduce.2.cloned.1.call-start = ((), (), s32[]{:S(2)}) async-start(), calls=%async_computation.4 | async-start | bytes 16777216 | tf_op jit(solution)/shard_map/psum | solution.py:42
  1193.7 369.9 %all-to-all-start.3 = ((bf16[64,128,2,1,512]{1,0,3,2,4:T(8,128)(2,1)}), bf16[64,128,2,1,512]{1,0,3,2,4:T(8,128)(2,1)}, u32[]{:S(2)}, u32[]{:S(2)}) async-start(bf16[64,128,2,1,512]{1,0,3,2,4:T(8,128)(2,1)} %copy.97), calls=%async_computation.3 | async-start | bytes 33554432 | tf_op jit(solution)/shard_map/all_to_all | solution.py:51
  1200.8 40.9 %copy-start.2 = (bf16[512,512]{1,0:T(8,128)(2,1)S(1)}, bf16[512,512]{1,0:T(8,128)(2,1)}, u32[]{:S(2)}) copy-start(bf16[512,512]{1,0:T(8,128)(2,1)} %copy-done.1) | copy-start | bytes 1572868
  1200.8 41.4 %copy-start.5 = (f32[512]{0:T(512)S(1)}, f32[512]{0:T(512)}, u32[]{:S(2)}) copy-start(f32[512]{0:T(512)} %param.13) | copy-start | bytes 6148
  1620.7 47.8 %copy-start.6 = (f32[128]{0:T(128)S(1)}, f32[128]{0:T(128)}, u32[]{:S(2)}) copy-start(f32[128]{0:T(128)} %dynamic_slice.13) | copy-start | bytes 1540
Sparse Core Ops, SparseCore 0:
  827.1 202.6 all-reduce.1
where the time goes:
time: 1800 us; the launch traced here: 1790 us
  blocking collectives  549 us (30%)
  local copies, waits for them, and re-layouts  498 us (28%)
  waiting for transfers between devices  271 us (15%)
  other arithmetic  257 us (14%)
  matrix products  175 us (10%)
  starting transfers between devices  20.2 us (1%)
    psum x1, blocking collectives, per_device(): total_x, total_z = lax.psum((part_x, part_z), ('pair', 'idx'))  360 us
    all_to_all x1, waiting for transfers between devices, per_device(): lax.all_to_all(part_two, 'idx', split_axis=4, concat_axis=1, tiled=True)  191 us
    all_to_all x1, blocking collectives, per_device(): part = lax.all_to_all(g2, 'pair', split_axis=1, concat_axis=0, tiled=True)  189 us
    psum x1, waiting for transfers between devices, per_device(): total_x, total_z = lax.psum((part_x, part_z), ('pair', 'idx'))  80.5 us
    another operation x1, other arithmetic  70.8 us
    unnamed x18, local copies, waits for them, and re-layouts  53.4 us
    dot_general x1, matrix products, per_device(): lax.dot_general(lmat, aux.reshape(rank, -1), (((0,), (0,)), ((), ())), pr...  50.2 us
    reshape x1, local copies, waits for them, and re-layouts, per_device(): term_k = jnp.einsum('km,imr->ikr', ham_b, g2.reshape(rows_loc, width, -1)...  48.5 us
  transfers between devices with their start and end apart: 4, of which 2 were waited for; matrix products, arithmetic and copies ran while one was open for 39% of the time, Pallas kernels for 0%

commit v1 on v0

--- a/solution.py
+++ b/solution.py
@@ -2,6 +2,22 @@
 import jax.numpy as jnp
 from jax import lax
 from jax.sharding import PartitionSpec as P
+
+
+def exchange_in_pairs(x, axis, split, join):
+    ways, here = (lax.axis_size(axis), lax.axis_index(axis))
+    width = x.shape[split] // ways
+    dims = list(x.shape)
+    dims[split] = width
+    height = dims[join]
+    dims[join] = height * ways
+    full = jnp.zeros(dims, x.dtype)
+    for mask in range(ways):
+        part = lax.dynamic_slice_in_dim(x, (here ^ mask) * width, width, axis=split)
+        if mask:
+            part = lax.ppermute(part, axis, [(d, d ^ mask) for d in range(ways)])
+        full = lax.dynamic_update_slice_in_dim(full, part, (here ^ mask) * height, axis=join)
+    return full
 
 
 def combine(total_x, total_z, rho_part):
@@ -48,7 +64,7 @@
         lmat, aux.reshape(rank, -1), (((0,), (0,)), ((), ())), preferred_element_type=jnp.float32
     )
     part_two = (factor_term.reshape(wide.shape) - ham_cols).astype(jnp.bfloat16)
-    term_two = lax.all_to_all(part_two, "idx", split_axis=4, concat_axis=1, tiled=True)
+    term_two = exchange_in_pairs(part_two, "idx", 4, 1)
     term_k = jnp.einsum(
         "km,imr->ikr", ham_b, g2.reshape(rows_loc, width, -1), preferred_element_type=jnp.float32
     ).reshape(g2.shape)

time: 1800 us -> 1880 us (1.044)
  the two profiles are of different devices: /device:TPU:0 before, /device:TPU:8 now
where the time goes in v1:
time: 1880 us; the launch traced here: 1860 us
  local copies, waits for them, and re-layouts  509 us (27%)
  blocking collectives  490 us (26%)
  waiting for transfers between devices  439 us (23%)
  other arithmetic  220 us (12%)
  matrix products  175 us (9%)
    psum x1, blocking collectives, per_device(): total_x, total_z = lax.psum((part_x, part_z), ('pair', 'idx'))  302 us
    ppermute x3, waiting for transfers between devices, exchange_in_pairs(): part = lax.ppermute(part, axis, [(d, d ^ mask) for d in range(ways)])  278 us
    all_to_all x1, blocking collectives, per_device(): part = lax.all_to_all(g2, 'pair', split_axis=1, concat_axis=0, tiled=True)  188 us
    psum x1, waiting for transfers between devices, per_device(): total_x, total_z = lax.psum((part_x, part_z), ('pair', 'idx'))  161 us
    another operation x1, other arithmetic  70.8 us
    unnamed x18, local copies, waits for them, and re-layouts  58.9 us
    dot_general x1, matrix products, per_device(): lax.dot_general(lmat, aux.reshape(rank, -1), (((0,), (0,)), ((), ())), pr...  50.2 us
    reshape x1, local copies, waits for them, and re-layouts, per_device(): term_k = jnp.einsum('km,imr->ikr', ham_b, g2.reshape(rows_loc, width, -1)...  48.6 us
  transfers between devices with their start and end apart: 6, of which 4 were waited for; matrix products, arithmetic and copies ran while one was open for 32% of the time, Pallas kernels for 0%

profile of v1, /device:TPU:8, one launch (start us, length us, event | category | flops | bytes accessed | tf_op | source)
XLA Modules:
  0.0 1864.7 jit_solution(3805267822345459376)
XLA Ops:
  6.5 17.1 copy.73
  29.4 187.7 %all_to_all.39 = bf16[64,512,2,1,128]{4,2,3,0,1:T(2,128)(2,1)} all-to-all(bf16[64,512,2,1,128]{4,2,3,0,1:T(2,128)(2,1)S(1)} %copy.73), channel_id=1, replica_groups=mesh['pair'=8,'idx'=4] {'pair'}, dimensions={1} | all-to-all | bytes 33554432 | tf_op jit(solution)/shard_map/all_to_all | solution.py:44
  224.3 40.8 %copy.94 = bf16[64,512,2,1,128]{1,4,2,0,3:T(8,128)(2,1)} copy(bf16[64,512,2,1,128]{4,2,3,1,0:T(2,128)(2,1)} %param.7) | data formatting | bytes 33554432 | tf_op jit(solution)/shard_map/reshape | solution.py:69
  265.1 17.5 convert_element_type.62
  284.7 17.2 fusion.17
  301.9 302.4 %psum.15 = f32[2048,2]{0,1:T(2,128)S(1)} all-reduce(f32[2048,2]{0,1:T(2,128)S(1)} %fusion.17), channel_id=1, replica_groups=mesh['pair'=8,'idx'=4] {'pair','idx'}, use_global_device_ids=true, to_apply=%region_1.0 | all-reduce | flops 4096 | bytes 32768 | tf_op jit(solution)/shard_map/psum | solution.py:58
  634.4 21.2 %fusion.24 = f32[512,64,256]{0,2,1:T(8,128)} fusion(bf16[64,512,256]{1,2,0:T(8,128)(2,1)} %bitcast.94, bf16[512,512]{1,0:T(8,128)(2,1)S(1)} %fusion.22), kind=kOutput, calls=%fused_computation.41 | convolution fusion | flops 8589934592 | bytes 50855936 | tf_op jit(solution)/shard_map/km,imr->ikr/dot_general | solution.py:68
  655.7 48.6 %copy.91 = f32[64,512,2,1,128]{4,2,3,1,0:T(2,128)} copy(f32[64,512,2,1,128]{1,4,2,0,3:T(8,128)} %bitcast.87) | data formatting | bytes 67108864 | tf_op jit(solution)/shard_map/reshape | solution.py:70
  706.2 18.2 copy.122
  724.4 27.7 %reshape.394 = bf16[512,16384]{1,0:T(8,128)(2,1)} reshape(bf16[8,64,64,2,1,128]{5,3,2,1,0,4:T(2,128)(2,1)} %bitcast.97) | data formatting | bytes 33554432 | tf_op jit(solution)/shard_map/reshape | solution.py:46
  752.2 42.7 %copy.123 = bf16[64,4,128,2,1,128]{5,1,3,2,0,4:T(4,128)(2,1)} copy(bf16[64,4,128,2,1,128]{5,3,0,2,1,4:T(2,128)(2,1)} %bitcast.9) | data formatting | bytes 33554432 | tf_op jit(solution)/shard_map/all_to_all | solution.py:49
  794.9 27.8 %reshape.408 = bf16[8192,1024]{1,0:T(8,128)(2,1)} reshape(bf16[64,128,2,1,4,128]{5,4,2,1,0,3:T(4,128)(2,1)} %bitcast.88) | data formatting | bytes 33554432 | tf_op jit(solution)/shard_map/reshape | solution.py:54
  822.6 44.8 %fusion.2 = f32[2048,1024]{1,0:T(8,128)} fusion(bf16[8192,1024]{1,0:T(8,128)(2,1)} %reshape.408, bf16[256,8,64,128]{3,2,1,0:T(8,128)(2,1)} %bitcast.90), kind=kOutput, calls=%fused_computation.2 | convolution fusion | flops 34359738368 | bytes 58720256 | tf_op jit(solution)/shard_map/dot_general | solution.py:54
  867.4 18.3 convolution_convert_fusion
  885.7 27.7 %reshape.395 = bf16[512,64,2,1,128]{4,2,1,0,3:T(2,128)(2,1)} reshape(bf16[512,16384]{1,0:T(8,128)(2,1)} %convolution_convert_fusion) | data formatting | bytes 33554432 | tf_op jit(solution)/shard_map/reshape | solution.py:47
  919.3 23.2 %convolution_bitcast_fusion = f32[16384,512]{0,1:T(8,128)} fusion(bf16[512,512]{1,0:T(8,128)(2,1)S(1)} %fusion.22, bf16[2048,8,4,128]{3,2,1,0:T(4,128)(2,1)} %bitcast.89), kind=kOutput, calls=%fused_computation.11 | convolution fusion | flops 8589934592 | bytes 50855936 | tf_op jit(solution)/shard_map/dot_general | solution.py:60
  942.5 33.4 %copy.84 = f32[16384,512]{1,0:T(8,128)} copy(f32[16384,512]{0,1:T(8,128)} %convolution_bitcast_fusion) | data formatting | bytes 67108864 | tf_op jit(solution)/shard_map/dot_general | solution.py:60
  975.9 39.1 %reshape.400 = f32[64,128,2,1,512]{4,2,1,0,3:T(2,128)} reshape(f32[16384,512]{1,0:T(8,128)} %copy.84) | data formatting | bytes 67108864 | tf_op jit(solution)/shard_map/reshape | solution.py:60
  1015.0 160.8 %all-reduce.2.cloned.1.call-done = f32[2048,1024]{1,0:T(8,128)} async-done(((f32[2048,1024]{1,0:T(8,128)}), f32[2048,1024]{1,0:T(8,128)}) %all-reduce.2.cloned.1.call-update) | async-done | bytes 8388624 | tf_op jit(solution)/shard_map/psum | solution.py:58
  1175.8 50.2 %fusion.14 = f32[128,8,64,128]{3,1,2,0:T(8,128)} fusion(bf16[256,8,64,128]{3,2,1,0:T(8,128)(2,1)} %bitcast.91, f32[2048,1024]{1,0:T(8,128)} %all-reduce.2.cloned.1.call-done, f32[2048,1024]{1,0:T(8,128)} %copy.83), kind=kOutput, calls=%fused_computation.25 | convolution fusion | flops 34363932672 | bytes 83886080 | tf_op jit(solution)/shard_map/dot_general | solution.py:63
  1226.0 27.5 %copy.97 = f32[128,8,64,128]{3,2,1,0:T(8,128)} copy(f32[128,8,64,128]{3,1,2,0:T(8,128)} %fusion.14) | data formatting | bytes 67108864
  1253.5 38.6 %copy.85 = f32[64,128,2,1,512]{4,2,1,0,3:T(2,128)} copy(f32[64,128,2,1,512]{1,0,4,2,3:T(8,128)} %bitcast.92) | data formatting | bytes 67108864 | tf_op jit(solution)/shard_map/reshape | solution.py:66
  1292.1 21.0 %subtract_convert_fusion = bf16[64,128,2,1,512]{4,2,1,0,3:T(2,128)(2,1)S(1)} fusion(f32[64,128,2,1,512]{4,2,1,0,3:T(2,128)} %copy.85, f32[64,128,2,1,512]{4,2,1,0,3:T(2,128)} %reshape.400), kind=kLoop, calls=%fused_computation.8 | loop fusion | flops 16777216 | bytes 83886080 | tf_op jit(solution)/shard_map/convert_element_type | solution.py:66
  1353.4 17.6 convert_bitcast_fusion
  1371.0 23.0 %copy.76 = f32[64,8,64,2,1,128]{5,3,2,1,0,4:T(2,128)} copy(f32[64,8,64,2,1,128]{5,3,2,0,1,4:T(2,128)} %convert_bitcast_fusion) | data formatting | bytes 67108864 | tf_op jit(solution)/shard_map/convert_element_type | solution.py:74
  1393.9 115.0 %collective-permute-done = bf16[64,128,2,1,128]{4,2,1,0,3:T(2,128)(2,1)} collective-permute-done((bf16[64,128,2,1,128]{4,2,1,0,3:T(2,128)(2,1)}, bf16[64,128,2,1,128]{4,2,1,0,3:T(2,128)(2,1)}, u32[]{:S(2)}, u32[]{:S(2)}) %collective-permute-start) | collective-permute-done | bytes 4194336 | tf_op jit(solution)/shard_map/ppermute | solution.py:18
  1519.3 84.1 %collective-permute-done.1 = bf16[64,128,2,1,128]{4,2,1,0,3:T(2,128)(2,1)} collective-permute-done((bf16[64,128,2,1,128]{4,2,1,0,3:T(2,128)(2,1)}, bf16[64,128,2,1,128]{4,2,1,0,3:T(2,128)(2,1)}, u32[]{:S(2)}, u32[]{:S(2)}) %collective-permute-start.1) | collective-permute-done | bytes 4194336 | tf_op jit(solution)/shard_map/ppermute | solution.py:18
  1613.8 78.9 %collective-permute-done.2 = bf16[64,128,2,1,128]{4,2,1,0,3:T(2,128)(2,1)} collective-permute-done((bf16[64,128,2,1,128]{4,2,1,0,3:T(2,128)(2,1)}, bf16[64,128,2,1,128]{4,2,1,0,3:T(2,128)(2,1)}, u32[]{:S(2)}, u32[]{:S(2)}) %collective-permute-start.2) | collective-permute-done | bytes 4194336 | tf_op jit(solution)/shard_map/ppermute | solution.py:18
  1692.7 10.4 bitcast_dynamic-update-slice_fusion
  1703.1 43.0 %add_subtract_fusion = f32[64,512,2,1,128]{4,2,3,1,0:T(2,128)} fusion(f32[64,512,2,1,128]{4,2,3,1,0:T(2,128)} %copy.91, f32[64,512,2,1,128]{4,2,3,1,0:T(2,128)} %bitcast.93, bf16[64,512,2,1,128]{4,2,3,1,0:T(2,128)(2,1)} %bitcast_dynamic-update-slice_fusion, f32[]{:T(128)S(6)} %convert.13, bf16[64,512,2,1,128]{4,2,3,1,0:T(2,128)(2,1)} %param.7), kind=kLoop, calls=%fused_computation.7 | loop fusion | flops 50331648 | bytes 134217728 | tf_op jit(solution)/shard_map/sub | solution.py:74
  1746.2 70.8 %fusion.13 = (bf16[64,512,1,1,128]{4,2,3,1,0:T(2,128)(2,1)S(1)}, bf16[64,512,1,1,128]{4,2,3,1,0:T(2,128)(2,1)}) fusion(f32[64,512,2,1,128]{4,2,3,1,0:T(2,128)} %add_subtract_fusion, f32[64,512,2,1,128]{4,2,3,1,0:T(2,128)} %convert_element_type.62, f32[128]{0:T(128)S(1)} %copy-done.6, f32[64,512]{1,0:T(8,128)S(1)} %copy-done.4), kind=kLoop, calls=%fused_computation.24 | loop fusion | flops 37748736 | bytes 84017664 | tf_op jit(solution)/shard_map/convert.4
  1816.9 40.7 %pad_maximum_fusion = bf16[64,512,2,1,128]{4,2,3,1,0:T(2,128)(2,1)} fusion(bf16[64,512,1,1,128]{4,2,3,1,0:T(2,128)(2,1)} %get-tuple-element.6, bf16[64,512,1,1,128]{4,2,3,1,0:T(2,128)(2,1)S(1)} %get-tuple-element.5), kind=kLoop, calls=%fused_computation.21 | loop fusion | flops 33554432 | bytes 33554432 | tf_op jit(solution)/shard_map/stack | solution.py:85
  (44 shorter events, 112.7 us)
Async XLA Ops:
  23.7 5.7 copy-start
  217.1 535.1 %all-to-all-start.2 = ((bf16[64,512,2,1,128]{4,2,3,0,1:T(2,128)(2,1)}), bf16[64,512,2,1,128]{4,2,3,0,1:T(2,128)(2,1)}, u32[]{:S(2)}, u32[]{:S(2)}) async-start(bf16[64,512,2,1,128]{4,2,3,0,1:T(2,128)(2,1)} %copy-done), calls=%async_computation.2 | async-start | bytes 33554432 | tf_op jit(solution)/shard_map/all_to_all | solution.py:49
  224.3 951.5 %all-reduce.2.cloned.1.call-start = ((), (), s32[]{:S(2)}) async-start(), calls=%async_computation.3 | async-start | bytes 16777216 | tf_op jit(solution)/shard_map/psum | solution.py:58
  265.0 17.5 copy-start.5
  610.3 18.2 copy-start.3
  610.3 19.5 %copy-start.2 = (f32[512,512]{1,0:T(8,128)S(1)}, f32[512,512]{1,0:T(8,128)}, u32[]{:S(2)}) copy-start(f32[512,512]{1,0:T(8,128)} %param.9) | copy-start | bytes 3145732
  913.4 440.0 %all-to-all-start.1 = ((bf16[512,64,2,1,128]{4,2,1,3,0:T(2,128)(2,1)}), bf16[512,64,2,1,128]{4,2,1,3,0:T(2,128)(2,1)}, u32[]{:S(2)}, u32[]{:S(2)}) async-start(bf16[512,64,2,1,128]{4,2,1,3,0:T(2,128)(2,1)} %bitcast.96), calls=%async_computation.1 | async-start | bytes 33554432 | tf_op jit(solution)/shard_map/all_to_all | solution.py:48
  1313.2 5.8 copy-start.1
  1329.4 179.5 %collective-permute-start = (bf16[64,128,2,1,128]{4,2,1,0,3:T(2,128)(2,1)}, bf16[64,128,2,1,128]{4,2,1,0,3:T(2,128)(2,1)}, u32[]{:S(2)}, u32[]{:S(2)}) collective-permute-start(bf16[64,128,2,1,128]{4,2,1,0,3:T(2,128)(2,1)} %get-tuple-element.9), channel_id=1, source_target_pairs={{0,1},{1,0},{2,3},{3,2},{4,5},{5,4},{6,7},{7,6},{8,9},{9,8},{10,11... | collective-permute-start | bytes 12582920 | tf_op jit(solution)/shard_map/ppermute | solution.py:18
  1330.0 273.4 %collective-permute-start.1 = (bf16[64,128,2,1,128]{4,2,1,0,3:T(2,128)(2,1)}, bf16[64,128,2,1,128]{4,2,1,0,3:T(2,128)(2,1)}, u32[]{:S(2)}, u32[]{:S(2)}) collective-permute-start(bf16[64,128,2,1,128]{4,2,1,0,3:T(2,128)(2,1)} %get-tuple-element.8), channel_id=1, source_target_pairs={{0,2},{1,3},{2,0},{3,1},{4,6},{5,7},{6,4},{7,5},{8,10},{9,11},{10,... | collective-permute-start | bytes 12582920 | tf_op jit(solution)/shard_map/ppermute | solution.py:18
  1332.4 360.3 %collective-permute-start.2 = (bf16[64,128,2,1,128]{4,2,1,0,3:T(2,128)(2,1)}, bf16[64,128,2,1,128]{4,2,1,0,3:T(2,128)(2,1)}, u32[]{:S(2)}, u32[]{:S(2)}) collective-permute-start(bf16[64,128,2,1,128]{4,2,1,0,3:T(2,128)(2,1)} %get-tuple-element.7), channel_id=1, source_target_pairs={{0,3},{1,2},{2,1},{3,0},{4,7},{5,6},{6,5},{7,4},{8,11},{9,10},{10,... | collective-permute-start | bytes 12582920 | tf_op jit(solution)/shard_map/ppermute | solution.py:18
  1703.1 43.0 %copy-start.4 = (f32[64,512]{1,0:T(8,128)S(1)}, f32[64,512]{1,0:T(8,128)}, u32[]{:S(2)}) copy-start(f32[64,512]{1,0:T(8,128)} %add_add_fusion) | copy-start | bytes 393220
  1703.1 43.0 %copy-start.6 = (f32[128]{0:T(128)S(1)}, f32[128]{0:T(128)}, u32[]{:S(2)}) copy-start(f32[128]{0:T(128)} %dynamic_slice.29) | copy-start | bytes 1540
Sparse Core Ops, SparseCore 0:
  867.6 308.2 all-reduce.1
